TPU v7x, 256 devices: a whole 4x4x8 slice. The times are simulated.
256 devices in a mesh: tok: 32 (over x, y, core), feat: 8 (over z).
Axes of the slice: x: 4, y: 4, z: 8, core: 2. Of those that a mesh axis runs over, the one named last changes fastest.
Arguments:
- inputs: bfloat16 [16384, 2048], P(('tok', 'feat'))
- norm_gain: float32 [2048], replicated, may hold values from 0.1 to 1.9
- w_in: bfloat16 [512, 8192], P('tok', 'feat'), may hold values from -0.25 to 0.25
- w_out: bfloat16 [512, 8192], P('tok', 'feat'), may hold values from -0.125 to 0.125
- block_index: int32 [64, 4], P('feat'), may hold values from 0 to 15, all different within a row
- segment_ids: int32 [16384], P(('tok', 'feat')), may hold values from 0 to 1023, never falling along the last dimension, each value on 1 to 24 neighbouring positions
- teacher_scores: float32 [1024], replicated, may hold values from -6 to 6
- upstream: bfloat16 [16384, 2048], P(('tok', 'feat')), may hold values from -6 to 6
- readout: float32 [2048], replicated, may hold values from -0.125 to 0.125
Outputs:
- layer_out: bfloat16 [16384, 2048], P(('tok', 'feat'))
- input_grad: bfloat16 [16384, 2048], P(('tok', 'feat'))
- grad_in: float32 [512, 8192], P('tok', 'feat')
- grad_out: float32 [512, 8192], P('tok', 'feat')
Inputs may be any that keep to these rules, and one draw needn't show every extreme that they name: `block_index`: each row names 4 different feature blocks; every feature block is named by some row. `segment_ids`: never falls along the tokens; every segment 0 to 1023 holds 1 to 24 tokens.
All inputs are finite; a program needn't handle non-finite values.
Results may differ from a plain program's by a relative error of at most 0.015.
Values may be sent and summed in bfloat16 or wider, within the bound.
A program may use at most 128 MiB of HBM per device.

v0:
```python
import math
import jax
import jax.numpy as jnp
from jax import lax
from jax.sharding import PartitionSpec as P

BLK = 128
EPS = 1e-06
LOSS_WEIGHT = 8.0


def gelu_tanh(values):
    return jax.nn.gelu(values, approximate=True)


def gelu_back(values, cotangent):
    return jax.vjp(gelu_tanh, values)[1](cotangent)[0]


def on_device(
    inputs, norm_gain, w_in, w_out, block_index, segment_ids, teacher_scores, upstream, readout
):
    local_tokens, model_width = inputs.shape
    blocks_here = w_in.shape[1] // BLK
    feature_blocks = model_width // BLK
    per_hidden = block_index.shape[1]
    total_tokens = local_tokens * lax.axis_size("tok") * lax.axis_size("feat")
    grad_scale = 1.0 / math.sqrt(total_tokens)
    inputs_wide = inputs.astype(jnp.float32)
    mean_square = jnp.mean(inputs_wide * inputs_wide, axis=1, keepdims=True)
    inv_rms = lax.rsqrt(mean_square + EPS)
    normed = (inputs_wide * inv_rms * norm_gain[None, :]).astype(jnp.bfloat16)
    w_in_all, w_out_all = (
        lax.all_gather(w_in, "tok", axis=0, tiled=True),
        lax.all_gather(w_out, "tok", axis=0, tiled=True),
    )
    picked_width = w_in_all.shape[0]
    w_in_blocks = w_in_all.reshape(picked_width, blocks_here, BLK)
    w_out_blocks = w_out_all.reshape(picked_width, blocks_here, BLK)
    normed_rows = lax.all_gather(normed, "feat", axis=0, tiled=True)
    group_rows = normed_rows.shape[0]
    one_hot = block_index[:, :, None] == jnp.arange(feature_blocks, dtype=jnp.int32)[None, None, :]
    sel_half = one_hot.astype(jnp.bfloat16)
    sel_wide = one_hot.astype(jnp.float32)

    def select(rows):
        blocks = rows.reshape(group_rows, feature_blocks, BLK)
        picked = jnp.einsum("rdc,jkd->rjkc", blocks, sel_half, preferred_element_type=jnp.float32)
        return picked.astype(jnp.bfloat16).reshape(group_rows, blocks_here, picked_width)

    def spread(terms):
        grouped = terms.reshape(group_rows, blocks_here, per_hidden, BLK)
        placed = jnp.einsum("rjkc,jkd->rdc", grouped, sel_wide, precision=lax.Precision.HIGHEST)
        return placed.reshape(group_rows, model_width)

    chosen = select(normed_rows)
    pre_act = jnp.einsum("rjm,mjc->rjc", chosen, w_in_blocks, preferred_element_type=jnp.float32)
    activated = gelu_tanh(pre_act).astype(jnp.bfloat16)
    out_terms_fwd = jnp.einsum(
        "rjc,mjc->rjm", activated, w_out_blocks, preferred_element_type=jnp.float32
    )
    branch = lax.psum_scatter(
        spread(out_terms_fwd).astype(jnp.bfloat16), "feat", scatter_dimension=0, tiled=True
    ).astype(jnp.float32)
    layer_out = (inputs_wide + branch).astype(jnp.bfloat16)
    token_score = jnp.dot(layer_out.astype(jnp.float32), readout, precision=lax.Precision.HIGHEST)
    segment_count = teacher_scores.shape[0]
    member = (segment_ids[:, None] == jnp.arange(segment_count, dtype=jnp.int32)[None, :]).astype(
        jnp.float32
    )
    score_sums = jnp.dot(token_score, member, precision=lax.Precision.HIGHEST)
    token_counts = jnp.sum(member, axis=0)
    score_sums, token_counts = lax.psum((score_sums, token_counts), ("tok", "feat"))
    misfit = score_sums / token_counts - teacher_scores
    token_coeff = 2.0 * LOSS_WEIGHT * jnp.sum(member * misfit[None, :], axis=1)
    cotangent_local = (
        upstream.astype(jnp.float32) + token_coeff[:, None] * readout[None, :]
    ).astype(jnp.bfloat16)
    cotangent_rows = lax.all_gather(cotangent_local, "feat", axis=0, tiled=True)
    chosen_grad = select(cotangent_rows)
    upper_grad = jnp.einsum(
        "rjm,mjc->rjc", chosen_grad, w_out_blocks, preferred_element_type=jnp.float32
    )
    pre_grad = gelu_back(pre_act, upper_grad).astype(jnp.bfloat16)

    def arrange(terms):
        return terms.reshape(picked_width, blocks_here * BLK) * grad_scale

    back_terms = jnp.einsum(
        "rjc,mjc->rjm", pre_grad, w_in_blocks, preferred_element_type=jnp.float32
    )
    out_terms = jnp.einsum(
        "rjm,rjc->mjc", chosen_grad, activated, preferred_element_type=jnp.float32
    )
    in_terms = jnp.einsum("rjm,rjc->mjc", chosen, pre_grad, preferred_element_type=jnp.float32)
    grad_out, grad_in = (
        lax.psum_scatter(
            arrange(out_terms).astype(jnp.bfloat16), "tok", scatter_dimension=0, tiled=True
        ).astype(jnp.float32),
        lax.psum_scatter(
            arrange(in_terms).astype(jnp.bfloat16), "tok", scatter_dimension=0, tiled=True
        ).astype(jnp.float32),
    )
    back_sum = lax.psum_scatter(
        spread(back_terms).astype(jnp.bfloat16), "feat", scatter_dimension=0, tiled=True
    ).astype(jnp.float32)
    scaled = back_sum * norm_gain[None, :]
    inner_mean = jnp.mean(scaled * inputs_wide, axis=1, keepdims=True)
    norm_back = inv_rms * scaled - inputs_wide * (inv_rms * inv_rms * inv_rms) * inner_mean
    input_grad = (cotangent_local.astype(jnp.float32) + norm_back).astype(jnp.bfloat16)
    return (layer_out, input_grad, grad_in, grad_out)


def solution(mesh):
    return jax.shard_map(
        on_device,
        mesh=mesh,
        in_specs=(
            P(("tok", "feat"), None),
            P(),
            P("tok", "feat"),
            P("tok", "feat"),
            P("feat", None),
            P(("tok", "feat")),
            P(),
            P(("tok", "feat"), None),
            P(),
        ),
        out_specs=(
            P(("tok", "feat"), None),
            P(("tok", "feat"), None),
            P("tok", "feat"),
            P("tok", "feat"),
        ),
        check_vma=False,
    )
```

profile of v0, /device:TPU:2, one launch (start us, length us, event | category | flops | bytes accessed | tf_op | source)
XLA Modules:
  0.0 581.6 jit_solution(5638336384249948303)
XLA Ops:
  11.7 49.1 %all-gather.7.cloned.1.call-done = bf16[512,1024]{1,0:T(8,128)(2,1)} async-done(((bf16[16,1024]{1,0:T(8,128)(2,1)}), bf16[512,1024]{1,0:T(8,128)(2,1)}) %all-gather.7.cloned.1.call-update) | async-done | bytes 1048592 | tf_op jit(solution)/shard_map/all_gather | solution.py:34
  62.3 48.1 %all-gather.9.cloned.1.call-done = bf16[512,1024]{1,0:T(8,128)(2,1)} async-done(((bf16[16,1024]{1,0:T(8,128)(2,1)}), bf16[512,1024]{1,0:T(8,128)(2,1)}) %all-gather.9.cloned.1.call-update) | async-done | bytes 1048592 | tf_op jit(solution)/shard_map/all_gather | solution.py:35
  111.8 41.5 %all-gather.5.cloned.1.call-done = bf16[512,2048]{1,0:T(8,128)(2,1)} async-done(((bf16[64,2048]{1,0:T(8,128)(2,1)}), bf16[512,2048]{1,0:T(8,128)(2,1)}) %all-gather.5.cloned.1.call-update) | async-done | bytes 2097168 | tf_op jit(solution)/shard_map/all_gather | solution.py:40
  153.3 2.2 copy.82
  159.5 4.5 fusion.47
  164.1 10.4 %copy.61 = f32[512,8,4,128]{3,1,2,0:T(8,128)} copy(f32[512,8,4,128]{0,3,2,1:T(8,128)} %bitcast.104) | data formatting | bytes 16777216 | tf_op jit(solution)/shard_map/reshape | solution.py:52
  174.5 5.6 bitcast_convert_fusion.1
  180.1 1.9 copy.107
  182.7 40.9 %reduce-scatter.5.cloned.1.call-done = bf16[64,2048]{1,0:T(8,128)(2,1)} async-done(((bf16[512,2048]{1,0:T(8,128)(2,1)}), bf16[64,2048]{1,0:T(8,128)(2,1)}) %reduce-scatter.5.cloned.1.call-update) | async-done | bytes 262160 | tf_op jit(solution)/shard_map/reduce_scatter | solution.py:62
  225.9 74.4 %all-reduce = (f32[1024]{0:T(1024)S(1)}, f32[1024]{0:T(1024)S(1)}) all-reduce(f32[1024]{0:T(1024)S(1)} %bitcast.124, f32[1024]{0:T(1024)S(1)} %convert_reduce_fusion), channel_id=1, replica_groups=mesh['tok'=32,'feat'=8] {'tok','feat'}, use_global_device_ids=true, to_apply=%region_2.0 | all-reduce | flops 2048 | bytes 16384 | tf_op jit(solution)/shard_map/psum | solution.py:73
  301.6 37.5 %all-gather.11.cloned.1.call-done = bf16[512,2048]{1,0:T(8,128)(2,1)} async-done(((bf16[64,2048]{1,0:T(8,128)(2,1)}), bf16[512,2048]{1,0:T(8,128)(2,1)}) %all-gather.11.cloned.1.call-update) | async-done | bytes 2097168 | tf_op jit(solution)/shard_map/all_gather | solution.py:79
  339.1 2.2 copy.84
  344.2 3.7 fusion.14
  347.9 3.6 multiply_convert_fusion.1
  351.5 2.4 copy.69
  354.0 6.2 %multiply_convert_fusion = bf16[8,128,512]{2,1,0:T(8,128)(2,1)} fusion(bf16[512,8,512]{2,1,0:T(8,128)(2,1)} %bitcast.116, f32[8,512,128]{2,1,0:T(8,128)S(1)} %copy-done.6), kind=kOutput, calls=%fused_computation.32 | convolution fusion | flops 542638080 | bytes 7340032 | tf_op jit(solution)/shard_map/rjm,rjc->mjc/dot_general | solution.py:92
  360.2 2.4 copy.72
  362.8 4.5 fusion.49
  367.4 10.5 %copy.66 = f32[512,8,4,128]{3,1,2,0:T(8,128)} copy(f32[512,8,4,128]{0,3,2,1:T(8,128)} %bitcast.103) | data formatting | bytes 16777216 | tf_op jit(solution)/shard_map/reshape | solution.py:52
  377.8 5.6 bitcast_convert_fusion
  385.4 52.5 %reduce-scatter.9.cloned.1.call-done = bf16[16,1024]{1,0:T(8,128)(2,1)} async-done(((bf16[512,1024]{1,0:T(8,128)(2,1)}), bf16[16,1024]{1,0:T(8,128)(2,1)}) %reduce-scatter.9.cloned.1.call-update) | async-done | bytes 32784 | tf_op jit(solution)/shard_map/reduce_scatter | solution.py:100
  439.2 87.3 %reduce-scatter.11.cloned.1.call-done = bf16[16,1024]{1,0:T(8,128)(2,1)} async-done(((bf16[512,1024]{1,0:T(8,128)(2,1)}), bf16[16,1024]{1,0:T(8,128)(2,1)}) %reduce-scatter.11.cloned.1.call-update) | async-done | bytes 32784 | tf_op jit(solution)/shard_map/reduce_scatter | solution.py:97
  527.9 43.7 %reduce-scatter.7.cloned.1.call-done = bf16[64,2048]{1,0:T(8,128)(2,1)} async-done(((bf16[512,2048]{1,0:T(8,128)(2,1)}), bf16[64,2048]{1,0:T(8,128)(2,1)}) %reduce-scatter.7.cloned.1.call-update) | async-done | bytes 262160 | tf_op jit(solution)/shard_map/reduce_scatter | solution.py:104
  572.8 2.0 fusion.32
  (73 shorter events, 24.7 us)
Async XLA Ops:
  7.2 53.6 %all-gather.7.cloned.1.call-start = ((), (), s32[]{:S(2)}) async-start(), calls=%async_computation.5 | async-start | bytes 1081344 | tf_op jit(solution)/shard_map/all_gather | solution.py:34
  7.9 102.4 %all-gather.9.cloned.1.call-start = ((), (), s32[]{:S(2)}) async-start(), calls=%async_computation.6 | async-start | bytes 1081344 | tf_op jit(solution)/shard_map/all_gather | solution.py:35
  8.6 144.7 %all-gather.5.cloned.1.call-start = ((), (), s32[]{:S(2)}) async-start(), calls=%async_computation.4 | async-start | bytes 2359296 | tf_op jit(solution)/shard_map/all_gather | solution.py:40
  11.6 212.0 %reduce-scatter.5.cloned.1.call-start = ((), (), s32[]{:S(2)}) async-start(), calls=%async_computation.7 | async-start | bytes 2359296 | tf_op jit(solution)/shard_map/reduce_scatter | solution.py:62
  153.3 2.2 copy-start.12
  157.6 2.0 copy-start.1
  159.5 4.6 copy-start.4
  182.0 41.6 %copy-start = (bf16[64,2048]{1,0:T(8,128)(2,1)S(1)}, bf16[64,2048]{1,0:T(8,128)(2,1)}, u32[]{:S(2)}) copy-start(bf16[64,2048]{1,0:T(8,128)(2,1)} %param.9) | copy-start | bytes 786436
  182.0 43.4 %copy-start.14 = (f32[2048]{0:T(1024)S(1)}, f32[2048]{0:T(1024)}, u32[]{:S(2)}) copy-start(f32[2048]{0:T(1024)} %param.17) | copy-start | bytes 24580
  182.0 118.3 %copy-start.15 = (f32[1024]{0:T(1024)S(1)}, f32[1024]{0:T(1024)}, u32[]{:S(2)}) copy-start(f32[1024]{0:T(1024)} %param.15) | copy-start | bytes 12292
  182.0 118.5 %copy-start.9 = (bf16[64,2048]{1,0:T(8,128)(2,1)S(1)}, bf16[64,2048]{1,0:T(8,128)(2,1)}, u32[]{:S(2)}) copy-start(bf16[64,2048]{1,0:T(8,128)(2,1)} %param.16) | copy-start | bytes 786436
  182.0 157.0 %all-gather.11.cloned.1.call-start = ((), (), s32[]{:S(2)}) async-start(), calls=%async_computation.8 | async-start | bytes 2359296 | tf_op jit(solution)/shard_map/all_gather | solution.py:79
  224.6 0.7 copy-start.11
  301.4 136.4 %reduce-scatter.9.cloned.1.call-start = ((), (), s32[]{:S(2)}) async-start(), calls=%async_computation.10 | async-start | bytes 1081344 | tf_op jit(solution)/shard_map/reduce_scatter | solution.py:100
  342.6 1.6 copy-start.5
  343.3 4.5 copy-start.3
  344.2 3.7 copy-start.2
  347.9 3.6 copy-start.7
  351.5 2.5 copy-start.6
  353.9 172.6 %reduce-scatter.11.cloned.1.call-start = ((), (), s32[]{:S(2)}) async-start(), calls=%async_computation.11 | async-start | bytes 1081344 | tf_op jit(solution)/shard_map/reduce_scatter | solution.py:97
  360.2 2.7 copy-start.8
  362.6 209.1 %reduce-scatter.7.cloned.1.call-start = ((), (), s32[]{:S(2)}) async-start(), calls=%async_computation.9 | async-start | bytes 2359296 | tf_op jit(solution)/shard_map/reduce_scatter | solution.py:104
  385.3 186.3 %copy-start.13 = (f32[2048]{0:T(1024)S(1)}, f32[2048]{0:T(1024)}, u32[]{:S(2)}) copy-start(f32[2048]{0:T(1024)} %param.10) | copy-start | bytes 24580
  385.4 187.4 %copy-start.10 = (bf16[64,2048]{1,0:T(8,128)(2,1)S(1)}, bf16[64,2048]{1,0:T(8,128)(2,1)}, u32[]{:S(2)}) copy-start(bf16[64,2048]{1,0:T(8,128)(2,1)} %param.16) | copy-start | bytes 786436
  (1 other events, 0.7 us)
Sparse Core Ops, SparseCore 0:
  10.5 50.1 all-gather.6
  63.3 46.9 all-gather.8
  112.7 40.5 all-gather.4
  182.1 41.4 reduce-scatter.4
  301.5 37.5 all-gather.10
  354.1 83.7 reduce-scatter.8
  441.6 84.8 reduce-scatter.10
  529.1 42.5 reduce-scatter.6
where the time goes:
time: 583 us; the launch traced here: 582 us
  waiting for transfers between devices  402 us (69%)
  blocking collectives  74.4 us (13%)
  local copies, waits for them, and re-layouts  41 us (7%)
  matrix products  38.3 us (7%)
  between operations  14.4 us (2%)
  other arithmetic  11 us (2%)
    reduce_scatter x1, waiting for transfers between devices, on_device(): lax.psum_scatter(arrange(out_terms).astype(jnp.bfloat16), 'tok', scatter_...  87.3 us
    psum x1, blocking collectives, on_device(): lax.psum((score_sums, token_counts), ('tok', 'feat'))  74.4 us
    reduce_scatter x1, waiting for transfers between devices, on_device(): lax.psum_scatter(arrange(in_terms).astype(jnp.bfloat16), 'tok', scatter_d...  52.5 us
    all_gather x1, waiting for transfers between devices, on_device(): lax.all_gather(w_in, 'tok', axis=0, tiled=True)  49.1 us
    all_gather x1, waiting for transfers between devices, on_device(): lax.all_gather(w_out, 'tok', axis=0, tiled=True)  48.1 us
    reduce_scatter x1, waiting for transfers between devices, on_device(): lax.psum_scatter(spread(back_terms).astype(jnp.bfloat16), 'feat', scatter...  43.7 us
    all_gather x1, waiting for transfers between devices, on_device(): normed_rows = lax.all_gather(normed, 'feat', axis=0, tiled=True)  41.5 us
    reduce_scatter x1, waiting for transfers between devices, on_device(): lax.psum_scatter(spread(out_terms_fwd).astype(jnp.bfloat16), 'feat', scat...  40.9 us
  transfers between devices with their start and end apart: 8, of which 8 were waited for; matrix products, arithmetic and copies ran while one was open for 7% of the time, Pallas kernels for 0%

commit v1 on v0

--- a/solution.py
+++ b/solution.py
@@ -7,6 +7,19 @@
 BLK = 128
 EPS = 1e-06
 LOSS_WEIGHT = 8.0
+
+
+def ring_gather(array, axis, dim):
+    ways = lax.axis_size(axis)
+    up = [(d, (d + 1) % ways) for d in range(ways)]
+    down = [(d, (d - 1) % ways) for d in range(ways)]
+    earlier, later = ([array], [array])
+    for _ in range(ways // 2):
+        earlier.append(lax.ppermute(earlier[-1], axis, up))
+    for _ in range((ways - 1) // 2):
+        later.append(lax.ppermute(later[-1], axis, down))
+    line = jnp.concatenate([*earlier[::-1], *later[1:]], axis=dim)
+    return jnp.roll(line, (lax.axis_index(axis) - ways // 2) * array.shape[dim], axis=dim)
 
 
 def gelu_tanh(values):
@@ -37,7 +50,7 @@
     picked_width = w_in_all.shape[0]
     w_in_blocks = w_in_all.reshape(picked_width, blocks_here, BLK)
     w_out_blocks = w_out_all.reshape(picked_width, blocks_here, BLK)
-    normed_rows = lax.all_gather(normed, "feat", axis=0, tiled=True)
+    normed_rows = ring_gather(normed, "feat", 0)
     group_rows = normed_rows.shape[0]
     one_hot = block_index[:, :, None] == jnp.arange(feature_blocks, dtype=jnp.int32)[None, None, :]
     sel_half = one_hot.astype(jnp.bfloat16)

time: 583 us -> 532 us (0.913)
  waiting for transfers between devices: 402 us -> 338 us
  starting transfers between devices: 0.72 us -> 12.7 us
    all_gather x1 -> x0, waiting for transfers between devices: 41.5 us -> none  [on_device(): normed_rows = lax.all_gather(normed, 'feat', axis=0, tiled=True)]
    all_gather x1, waiting for transfers between devices: 49.1 us -> 7.75 us  [on_device(): lax.all_gather(w_in, 'tok', axis=0, tiled=True)]
    reduce_scatter x1, waiting for transfers between devices: 87.3 us -> 51.3 us  [on_device(): lax.psum_scatter(arrange(out_terms).astype(jnp.bfloat16), 'tok', scatter_...]
    reduce_scatter x1, waiting for transfers between devices: 52.5 us -> 87.2 us  [on_device(): lax.psum_scatter(arrange(in_terms).astype(jnp.bfloat16), 'tok', scatter_d...]
    ppermute x0 -> x7, waiting for transfers between devices: none -> 24.3 us  [the longest x4 24.3 us: ring_gather(): earlier.append(lax.ppermute(earlier[-1], axis, up))]
    ppermute x0 -> x7, starting transfers between devices: none -> 12 us  [the longest x3 9.96 us: ring_gather(): later.append(lax.ppermute(later[-1], axis, down))]
  transfers between devices with their start and end apart: 8 -> 14, of which waited for: 8 -> 11; matrix products, arithmetic and copies ran while one was open for 7% -> 9% of each run, Pallas kernels for 0% -> 0%
where the time goes in v1:
time: 532 us; the launch traced here: 531 us
  waiting for transfers between devices  338 us (64%)
  blocking collectives  74.4 us (14%)
  matrix products  41.3 us (8%)
  local copies, waits for them, and re-layouts  38.6 us (7%)
  between operations  14.6 us (3%)
  starting transfers between devices  12.7 us (2%)
  other arithmetic  11.5 us (2%)
    reduce_scatter x1, waiting for transfers between devices, on_device(): lax.psum_scatter(arrange(in_terms).astype(jnp.bfloat16), 'tok', scatter_d...  87.2 us
    psum x1, blocking collectives, on_device(): lax.psum((score_sums, token_counts), ('tok', 'feat'))  74.4 us
    reduce_scatter x1, waiting for transfers between devices, on_device(): lax.psum_scatter(arrange(out_terms).astype(jnp.bfloat16), 'tok', scatter_...  51.3 us
    reduce_scatter x1, waiting for transfers between devices, on_device(): lax.psum_scatter(spread(back_terms).astype(jnp.bfloat16), 'feat', scatter...  43.8 us
    all_gather x1, waiting for transfers between devices, on_device(): lax.all_gather(w_out, 'tok', axis=0, tiled=True)  43.1 us
    reduce_scatter x1, waiting for transfers between devices, on_device(): lax.psum_scatter(spread(out_terms_fwd).astype(jnp.bfloat16), 'feat', scat...  42.5 us
    all_gather x1, waiting for transfers between devices, on_device(): cotangent_rows = lax.all_gather(cotangent_local, 'feat', axis=0, tiled=True)  37.4 us
    ppermute x4, waiting for transfers between devices, ring_gather(): earlier.append(lax.ppermute(earlier[-1], axis, up))  24.3 us
  transfers between devices with their start and end apart: 14, of which 11 were waited for; matrix products, arithmetic and copies ran while one was open for 9% of the time, Pallas kernels for 0%

profile of v1, /device:TPU:2, one launch (start us, length us, event | category | flops | bytes accessed | tf_op | source)
XLA Modules:
  0.0 531.2 jit_solution(3993007331588601763)
XLA Ops:
  12.2 10.2 %collective-permute-done = bf16[64,2048]{1,0:T(8,128)(2,1)S(1)} collective-permute-done((bf16[64,2048]{1,0:T(8,128)(2,1)S(1)}, bf16[64,2048]{1,0:T(8,128)(2,1)S(1)}, u32[]{:S(2)}, u32[]{:S(2)}) %collective-permute-start) | collective-permute-done | bytes 262176 | tf_op jit(solution)/shard_map/ppermute | solution.py:18
  22.4 3.2 collective-permute-start.4
  25.7 5.4 %collective-permute-done.1 = bf16[64,2048]{1,0:T(8,128)(2,1)S(1)} collective-permute-done((bf16[64,2048]{1,0:T(8,128)(2,1)S(1)}, bf16[64,2048]{1,0:T(8,128)(2,1)S(1)}, u32[]{:S(2)}, u32[]{:S(2)}) %collective-permute-start.1) | collective-permute-done | bytes 262176 | tf_op jit(solution)/shard_map/ppermute | solution.py:18
  31.1 3.2 collective-permute-start.5
  34.3 4.6 collective-permute-done.2
  39.0 3.5 collective-permute-start.6
  42.5 4.0 collective-permute-done.3
  53.0 7.8 %all-gather.4.cloned.1.call-done = bf16[512,1024]{1,0:T(8,128)(2,1)} async-done(((bf16[16,1024]{1,0:T(8,128)(2,1)}), bf16[512,1024]{1,0:T(8,128)(2,1)}) %all-gather.4.cloned.1.call-update) | async-done | bytes 1048592 | tf_op jit(solution)/shard_map/all_gather | solution.py:47
  62.3 4.9 fusion.6
  67.2 43.1 %all-gather.6.cloned.1.call-done = bf16[512,1024]{1,0:T(8,128)(2,1)} async-done(((bf16[16,1024]{1,0:T(8,128)(2,1)}), bf16[512,1024]{1,0:T(8,128)(2,1)}) %all-gather.6.cloned.1.call-update) | async-done | bytes 1048592 | tf_op jit(solution)/shard_map/all_gather | solution.py:48
  111.8 6.1 %fusion.47 = f32[8,512,512]{1,2,0:T(8,128)} fusion(bf16[512,8,128]{0,2,1:T(8,128)(2,1)S(1)} %bitcast.118, f32[8,512,128]{2,1,0:T(8,128)} %fusion.6), kind=kOutput, calls=%fused_computation.85 | convolution fusion | flops 541589504 | bytes 11534336 | tf_op jit(solution)/shard_map/rjc,mjc->rjm/dot_general | solution.py:72
  118.0 10.4 %copy.61 = f32[512,8,4,128]{3,1,2,0:T(8,128)} copy(f32[512,8,4,128]{0,3,2,1:T(8,128)} %bitcast.105) | data formatting | bytes 16777216 | tf_op jit(solution)/shard_map/reshape | solution.py:65
  128.4 5.6 %bitcast_convert_fusion.1 = bf16[16,512,128]{2,0,1:T(8,128)(2,1)S(1)} fusion(f32[512,8,4,128]{3,1,2,0:T(8,128)} %copy.61, s32[8,4]{0,1:T(4,128)S(1)} %copy-done.8), kind=kOutput, calls=%fused_computation.1 | convolution fusion | flops 403702272 | bytes 10485888 | tf_op jit(solution)/shard_map/rjkc,jkd->rdc/dot_general | solution.py:66
  136.1 42.5 %reduce-scatter.5.cloned.1.call-done = bf16[64,2048]{1,0:T(8,128)(2,1)} async-done(((bf16[512,2048]{1,0:T(8,128)(2,1)}), bf16[64,2048]{1,0:T(8,128)(2,1)}) %reduce-scatter.5.cloned.1.call-update) | async-done | bytes 262160 | tf_op jit(solution)/shard_map/reduce_scatter | solution.py:75
  180.9 74.4 %all-reduce = (f32[1024]{0:T(1024)S(1)}, f32[1024]{0:T(1024)S(1)}) all-reduce(f32[1024]{0:T(1024)S(1)} %bitcast.124, f32[1024]{0:T(1024)S(1)} %convert_reduce_fusion), channel_id=1, replica_groups=mesh['tok'=32,'feat'=8] {'tok','feat'}, use_global_device_ids=true, to_apply=%region_2.3 | all-reduce | flops 2048 | bytes 16384 | tf_op jit(solution)/shard_map/psum | solution.py:86
  256.7 37.4 %all-gather.8.cloned.1.call-done = bf16[512,2048]{1,0:T(8,128)(2,1)} async-done(((bf16[64,2048]{1,0:T(8,128)(2,1)}), bf16[512,2048]{1,0:T(8,128)(2,1)}) %all-gather.8.cloned.1.call-update) | async-done | bytes 2097168 | tf_op jit(solution)/shard_map/all_gather | solution.py:92
  299.2 3.0 multiply_convert_fusion
  303.7 5.6 %fusion.14 = bf16[512,8,128]{2,0,1:T(8,128)(2,1)S(1)} fusion(f32[8,512,128]{2,1,0:T(8,128)} %fusion.6, bf16[512,8,128]{0,2,1:T(8,128)(2,1)S(1)} %bitcast.119, bf16[512,8,512]{2,1,0:T(8,128)(2,1)} %bitcast.117), kind=kOutput, calls=%fused_computation.22 | convolution fusion | flops 547356672 | bytes 8388608 | tf_op jit(solution)/shard_map/rjm,mjc->rjc/dot_general | solution.py:94
  313.7 4.5 fusion.49
  318.2 10.5 %copy.66 = f32[512,8,4,128]{3,1,2,0:T(8,128)} copy(f32[512,8,4,128]{0,3,2,1:T(8,128)} %bitcast.104) | data formatting | bytes 16777216 | tf_op jit(solution)/shard_map/reshape | solution.py:65
  328.7 5.6 %bitcast_convert_fusion = bf16[16,512,128]{2,0,1:T(8,128)(2,1)S(1)} fusion(f32[512,8,4,128]{3,1,2,0:T(8,128)} %copy.66, s32[8,4]{0,1:T(4,128)S(1)} %copy-done.8), kind=kOutput, calls=%fused_computation | convolution fusion | flops 403702272 | bytes 10485888 | tf_op jit(solution)/shard_map/rjkc,jkd->rdc/dot_general | solution.py:66
  336.2 51.3 %reduce-scatter.11.cloned.1.call-done = bf16[16,1024]{1,0:T(8,128)(2,1)} async-done(((bf16[512,1024]{1,0:T(8,128)(2,1)}), bf16[16,1024]{1,0:T(8,128)(2,1)}) %reduce-scatter.11.cloned.1.call-update) | async-done | bytes 32784 | tf_op jit(solution)/shard_map/reduce_scatter | solution.py:110
  388.9 87.2 %reduce-scatter.9.cloned.1.call-done = bf16[16,1024]{1,0:T(8,128)(2,1)} async-done(((bf16[512,1024]{1,0:T(8,128)(2,1)}), bf16[16,1024]{1,0:T(8,128)(2,1)}) %reduce-scatter.9.cloned.1.call-update) | async-done | bytes 32784 | tf_op jit(solution)/shard_map/reduce_scatter | solution.py:113
  477.4 43.8 %reduce-scatter.7.cloned.1.call-done = bf16[64,2048]{1,0:T(8,128)(2,1)} async-done(((bf16[512,2048]{1,0:T(8,128)(2,1)}), bf16[64,2048]{1,0:T(8,128)(2,1)}) %reduce-scatter.7.cloned.1.call-update) | async-done | bytes 262160 | tf_op jit(solution)/shard_map/reduce_scatter | solution.py:117
  (91 shorter events, 38.7 us)
Async XLA Ops:
  7.2 40.8 %copy-start = (bf16[64,2048]{1,0:T(8,128)(2,1)S(1)}, bf16[64,2048]{1,0:T(8,128)(2,1)}, u32[]{:S(2)}) copy-start(bf16[64,2048]{1,0:T(8,128)(2,1)} %param.9) | copy-start | bytes 786436
  7.2 40.8 %copy-start.7 = (f32[2048]{0:T(1024)S(1)}, f32[2048]{0:T(1024)}, u32[]{:S(2)}) copy-start(f32[2048]{0:T(1024)} %param.10) | copy-start | bytes 24580
  7.2 53.6 %all-gather.4.cloned.1.call-start = ((), (), s32[]{:S(2)}) async-start(), calls=%async_computation.4 | async-start | bytes 1081344 | tf_op jit(solution)/shard_map/all_gather | solution.py:47
  7.9 102.4 %all-gather.6.cloned.1.call-start = ((), (), s32[]{:S(2)}) async-start(), calls=%async_computation.5 | async-start | bytes 1081344 | tf_op jit(solution)/shard_map/all_gather | solution.py:48
  10.2 12.2 %collective-permute-start = (bf16[64,2048]{1,0:T(8,128)(2,1)S(1)}, bf16[64,2048]{1,0:T(8,128)(2,1)S(1)}, u32[]{:S(2)}, u32[]{:S(2)}) collective-permute-start(bf16[64,2048]{1,0:T(8,128)(2,1)S(1)} %fusion.27), channel_id=1, source_target_pairs={{0,1},{1,2},{2,3},{3,4},{4,5},{5,6},{6,7},{7,0},{8,9},{9,10},{10,1... | collective-permute-start | bytes 786440 | tf_op jit(solution)/shard_map/ppermute | solution.py:18
  22.4 8.7 %collective-permute-start.1 = (bf16[64,2048]{1,0:T(8,128)(2,1)S(1)}, bf16[64,2048]{1,0:T(8,128)(2,1)S(1)}, u32[]{:S(2)}, u32[]{:S(2)}) collective-permute-start(bf16[64,2048]{1,0:T(8,128)(2,1)S(1)} %collective-permute-done), channel_id=1, source_target_pairs={{0,1},{1,2},{2,3},{3,4},{4,5},{5,6},{6,7},{7,0},{8,9},{9,10},{10,1... | collective-permute-start | bytes 786440 | tf_op jit(solution)/shard_map/ppermute | solution.py:18
  22.4 8.7 %collective-permute-start.4 = (bf16[64,2048]{1,0:T(8,128)(2,1)S(1)}, bf16[64,2048]{1,0:T(8,128)(2,1)S(1)}, u32[]{:S(2)}, u32[]{:S(2)}) collective-permute-start(bf16[64,2048]{1,0:T(8,128)(2,1)S(1)} %fusion.27), channel_id=1, source_target_pairs={{0,7},{1,0},{2,1},{3,2},{4,3},{5,4},{6,5},{7,6},{8,15},{9,8},{10,9... | collective-permute-start | bytes 786440 | tf_op jit(solution)/shard_map/ppermute | solution.py:20
  31.1 7.8 %collective-permute-start.2 = (bf16[64,2048]{1,0:T(8,128)(2,1)S(1)}, bf16[64,2048]{1,0:T(8,128)(2,1)S(1)}, u32[]{:S(2)}, u32[]{:S(2)}) collective-permute-start(bf16[64,2048]{1,0:T(8,128)(2,1)S(1)} %collective-permute-done.1), channel_id=1, source_target_pairs={{0,1},{1,2},{2,3},{3,4},{4,5},{5,6},{6,7},{7,0},{8,9},{9,10},{10,1... | collective-permute-start | bytes 786440 | tf_op jit(solution)/shard_map/ppermute | solution.py:18
  31.1 7.9 %collective-permute-start.5 = (bf16[64,2048]{1,0:T(8,128)(2,1)S(1)}, bf16[64,2048]{1,0:T(8,128)(2,1)S(1)}, u32[]{:S(2)}, u32[]{:S(2)}) collective-permute-start(bf16[64,2048]{1,0:T(8,128)(2,1)S(1)} %collective-permute-done.4), channel_id=1, source_target_pairs={{0,7},{1,0},{2,1},{3,2},{4,3},{5,4},{6,5},{7,6},{8,15},{9,8},{10,9... | collective-permute-start | bytes 786440 | tf_op jit(solution)/shard_map/ppermute | solution.py:20
  38.9 7.6 %collective-permute-start.3 = (bf16[64,2048]{1,0:T(8,128)(2,1)S(1)}, bf16[64,2048]{1,0:T(8,128)(2,1)S(1)}, u32[]{:S(2)}, u32[]{:S(2)}) collective-permute-start(bf16[64,2048]{1,0:T(8,128)(2,1)S(1)} %collective-permute-done.2), channel_id=1, source_target_pairs={{0,1},{1,2},{2,3},{3,4},{4,5},{5,6},{6,7},{7,0},{8,9},{9,10},{10,1... | collective-permute-start | bytes 786440 | tf_op jit(solution)/shard_map/ppermute | solution.py:18
  39.0 139.7 %reduce-scatter.5.cloned.1.call-start = ((), (), s32[]{:S(2)}) async-start(), calls=%async_computation.6 | async-start | bytes 2359296 | tf_op jit(solution)/shard_map/reduce_scatter | solution.py:75
  39.0 8.7 %collective-permute-start.6 = (bf16[64,2048]{1,0:T(8,128)(2,1)S(1)}, bf16[64,2048]{1,0:T(8,128)(2,1)S(1)}, u32[]{:S(2)}, u32[]{:S(2)}) collective-permute-start(bf16[64,2048]{1,0:T(8,128)(2,1)S(1)} %collective-permute-done.5), channel_id=1, source_target_pairs={{0,7},{1,0},{2,1},{3,2},{4,3},{5,4},{6,5},{7,6},{8,15},{9,8},{10,9... | collective-permute-start | bytes 786440 | tf_op jit(solution)/shard_map/ppermute | solution.py:20
  134.0 2.0 copy-start.11
  134.0 46.3 %copy-start.9 = (f32[2048]{0:T(1024)S(1)}, f32[2048]{0:T(1024)}, u32[]{:S(2)}) copy-start(f32[2048]{0:T(1024)} %param.17) | copy-start | bytes 24580
  134.0 121.4 %copy-start.10 = (f32[1024]{0:T(1024)S(1)}, f32[1024]{0:T(1024)}, u32[]{:S(2)}) copy-start(f32[1024]{0:T(1024)} %param.15) | copy-start | bytes 12292
  134.0 121.6 %copy-start.4 = (bf16[64,2048]{1,0:T(8,128)(2,1)S(1)}, bf16[64,2048]{1,0:T(8,128)(2,1)}, u32[]{:S(2)}) copy-start(bf16[64,2048]{1,0:T(8,128)(2,1)} %param.16) | copy-start | bytes 786436
  136.0 158.2 %all-gather.8.cloned.1.call-start = ((), (), s32[]{:S(2)}) async-start(), calls=%async_computation.7 | async-start | bytes 2359296 | tf_op jit(solution)/shard_map/all_gather | solution.py:92
  256.5 131.0 %reduce-scatter.11.cloned.1.call-start = ((), (), s32[]{:S(2)}) async-start(), calls=%async_computation.10 | async-start | bytes 1081344 | tf_op jit(solution)/shard_map/reduce_scatter | solution.py:110
  297.6 1.6 copy-start.3
  298.4 3.9 copy-start.2
  303.6 172.4 %reduce-scatter.9.cloned.1.call-start = ((), (), s32[]{:S(2)}) async-start(), calls=%async_computation.9 | async-start | bytes 1081344 | tf_op jit(solution)/shard_map/reduce_scatter | solution.py:113
  303.7 5.6 %copy-start.1 = (bf16[512,8,4,128]{3,1,2,0:T(8,128)(2,1)S(1)}, bf16[512,8,4,128]{3,1,2,0:T(8,128)(2,1)}, u32[]{:S(2)}) copy-start(bf16[512,8,4,128]{3,1,2,0:T(8,128)(2,1)} %copy.105) | copy-start | bytes 12582916
  313.4 207.8 %reduce-scatter.7.cloned.1.call-start = ((), (), s32[]{:S(2)}) async-start(), calls=%async_computation.8 | async-start | bytes 2359296 | tf_op jit(solution)/shard_map/reduce_scatter | solution.py:117
  334.3 188.0 %copy-start.5 = (bf16[64,2048]{1,0:T(8,128)(2,1)S(1)}, bf16[64,2048]{1,0:T(8,128)(2,1)}, u32[]{:S(2)}) copy-start(bf16[64,2048]{1,0:T(8,128)(2,1)} %param.16) | copy-start | bytes 786436
  (2 other events, 1.6 us)
Sparse Core Ops, SparseCore 0:
  10.6 50.1 all-gather.3
  63.3 46.9 all-gather.5
  136.1 42.5 reduce-scatter.4
  256.6 37.5 all-gather.7
  303.7 83.7 reduce-scatter.10
  391.1 84.8 reduce-scatter.8
  478.6 42.5 reduce-scatter.6
